TPU v7x, 32 devices: a whole 2x2x4 slice. The times are simulated.
32 devices in a mesh: groups: 2 (over y), seq: 4 (over z), mp: 4 (over x, core).
Axes of the slice: x: 2, y: 2, z: 4, core: 2. Of those that a mesh axis runs over, the one named last changes fastest.
Arguments:
- node_vectors: bfloat16 [1024, 2048], P(('groups', 'seq'), 'mp'), parts along dimension 0, may hold values from -6 to 6
- standardize_multiplier: float32 [2048], replicated, may hold values from 0.1 to 1.9
- probe_matrix: bfloat16 [2048, 1024], P(None, 'mp'), may hold values from -1 to 1
- lookup_matrix: bfloat16 [2048, 1024], P(None, 'mp'), may hold values from -1 to 1
- content_matrix: bfloat16 [2048, 1024], P(None, 'mp'), may hold values from -0.125 to 0.125
- softness_per_group: float32 [8], P('mp'), may hold values from 0.5 to 12
- exit_matrix: bfloat16 [1024, 2048], P('mp'), may hold values from -0.1875 to 0.1875
Outputs:
- mixed: bfloat16 [1024, 2048], P(('groups', 'seq'), 'mp'), parts along dimension 0
There are 2 independent parts, one for each index of `groups`. A program takes and returns all parts, laid end to end along the dimension named above; an argument that names none is the same for every part. Nothing has to cross between parts.
All inputs are finite; a program needn't handle non-finite values.
Results may differ from a plain program's by a relative error of at most 0.011.
Values may be sent and summed in bfloat16 or wider, within the bound.
A program may use at most 64 MiB of HBM per device.

v0:
```python
import math
import jax
import jax.numpy as jnp
from jax import lax
from jax.sharding import PartitionSpec as P


def attend(state_in, blocks, query_heads, inverse_root_span, resident_groups, channel_span):
    running_max, running_sum, weighted = state_in
    key_block, value_block = blocks
    count = key_block.shape[0]
    key_heads = key_block.reshape(count, resident_groups, channel_span)
    value_heads = value_block.reshape(count, resident_groups, channel_span)
    scores = (
        jnp.einsum("rhd,nhd->hrn", query_heads, key_heads, preferred_element_type=jnp.float32)
        * inverse_root_span[:, None, None]
    )
    new_max = jnp.max(scores, axis=-1)
    rescale = jnp.exp(running_max - new_max)
    weights = jnp.exp(scores - new_max[:, :, None])
    running_sum = running_sum * rescale + jnp.sum(weights, axis=-1)
    update = jnp.einsum(
        "hrn,nhd->hrd",
        weights.astype(jnp.bfloat16),
        value_heads,
        preferred_element_type=jnp.float32,
    )
    weighted = weighted * rescale[:, :, None] + update
    return (new_max, running_sum, weighted)


def per_device(
    node_vectors,
    standardize_multiplier,
    probe_matrix,
    lookup_matrix,
    content_matrix,
    softness_per_group,
    exit_matrix,
):
    full_rows = lax.all_gather(node_vectors, "mp", axis=1, tiled=True)
    widened = full_rows.astype(jnp.float32)
    average = jnp.mean(widened, axis=-1, keepdims=True)
    centered = widened - average
    variance = jnp.mean(centered * centered, axis=-1, keepdims=True)
    normed = (centered * lax.rsqrt(variance + 1e-05) * standardize_multiplier).astype(jnp.bfloat16)
    queries = jnp.dot(normed, probe_matrix, preferred_element_type=jnp.float32).astype(jnp.bfloat16)
    key_rows = jnp.dot(normed, lookup_matrix, preferred_element_type=jnp.float32).astype(
        jnp.bfloat16
    )
    value_rows = jnp.dot(normed, content_matrix, preferred_element_type=jnp.float32).astype(
        jnp.bfloat16
    )
    resident_groups = softness_per_group.shape[0]
    head_cols = queries.shape[1]
    channel_span = head_cols // resident_groups
    token_count = queries.shape[0]
    query_heads = queries.reshape(token_count, resident_groups, channel_span)
    inverse_root_span = softness_per_group / math.sqrt(channel_span)
    initial = (
        jnp.full((resident_groups, token_count), -jnp.inf, jnp.float32),
        jnp.zeros((resident_groups, token_count), jnp.float32),
        jnp.zeros((resident_groups, token_count, channel_span), jnp.float32),
    )
    final = attend(
        initial,
        (
            lax.all_gather(key_rows, "seq", axis=0, tiled=True),
            lax.all_gather(value_rows, "seq", axis=0, tiled=True),
        ),
        query_heads,
        inverse_root_span,
        resident_groups,
        channel_span,
    )
    heads_out = (
        (final[2] / final[1][:, :, None])
        .transpose(1, 0, 2)
        .reshape(token_count, head_cols)
        .astype(jnp.bfloat16)
    )
    partial_sums = jnp.dot(heads_out, exit_matrix, preferred_element_type=jnp.float32)
    summed = lax.psum_scatter(
        partial_sums.astype(jnp.bfloat16), "mp", scatter_dimension=1, tiled=True
    ).astype(jnp.float32)
    return (node_vectors.astype(jnp.float32) + summed).astype(jnp.bfloat16)


def solution(mesh):
    return jax.shard_map(
        per_device,
        mesh=mesh,
        in_specs=(
            P(("groups", "seq"), "mp"),
            P(),
            P(None, "mp"),
            P(None, "mp"),
            P(None, "mp"),
            P("mp"),
            P("mp", None),
        ),
        out_specs=P(("groups", "seq"), "mp"),
        check_vma=False,
    )
```

profile of v0, /device:TPU:0, one launch (start us, length us, event | category | flops | bytes accessed | tf_op | source)
XLA Modules:
  0.0 81.6 jit_solution(14585379958456140718)
XLA Ops:
  6.5 0.0 copy-start
  6.5 0.0 reduce-scatter.2.cloned.1.call-start
  6.5 0.8 broadcast_multiply_fusion
  7.3 8.8 %all_gather.9 = bf16[128,2048]{1,0:T(8,128)(2,1)S(1)} all-gather(bf16[128,512]{1,0:T(8,128)(2,1)} %param.7), channel_id=1, replica_groups=mesh['groups'=2,'seq'=4,'mp'=4] {'mp'}, dimensions={1}, use_global_device_ids=true | all-gather | bytes 655360 | tf_op jit(solution)/shard_map/all_gather | solution.py:41
  16.2 0.2 convert_reduce_fusion
  16.4 0.3 fusion.6
  16.7 0.0 copy-done.2
  16.7 0.4 copy-done.5
  17.1 0.4 convolution_convert_fusion.2
  17.4 0.9 %copy-done.3 = bf16[2048,256]{1,0:T(8,128)(2,1)S(1)} copy-done((bf16[2048,256]{1,0:T(8,128)(2,1)S(1)}, bf16[2048,256]{1,0:T(8,128)(2,1)}, u32[]{:S(2)}) %copy-start.3) | copy-done | bytes 1048600
  18.3 0.4 convolution_convert_fusion.1
  18.6 0.9 %copy-done.4 = bf16[2048,256]{1,0:T(8,128)(2,1)S(1)} copy-done((bf16[2048,256]{1,0:T(8,128)(2,1)S(1)}, bf16[2048,256]{1,0:T(8,128)(2,1)}, u32[]{:S(2)}) %copy-start.4) | copy-done | bytes 1048600
  19.5 0.4 fusion.5
  19.9 14.1 %all_gather.11 = bf16[512,256]{1,0:T(8,128)(2,1)S(1)} all-gather(bf16[128,256]{1,0:T(8,128)(2,1)S(1)} %convolution_convert_fusion.1), channel_id=1, replica_groups=mesh['groups'=2,'seq'=4,'mp'=4] {'seq'}, dimensions={0}, use_global_device_ids=true | all-gather | bytes 327680 | tf_op jit(solution)/shard_map/all_gather | solution.py:69
  34.0 0.1 copy.11
  34.1 14.6 %all_gather.10 = bf16[512,256]{1,0:T(8,128)(2,1)S(1)} all-gather(bf16[128,256]{1,0:T(8,128)(2,1)S(1)} %convolution_convert_fusion.2), channel_id=1, replica_groups=mesh['groups'=2,'seq'=4,'mp'=4] {'seq'}, dimensions={0}, use_global_device_ids=true | all-gather | bytes 327680 | tf_op jit(solution)/shard_map/all_gather | solution.py:68
  48.7 0.3 fusion.20
  49.1 0.2 fusion.9
  49.3 0.3 fusion.4
  49.6 1.1 %convolution_convert_fusion = bf16[128,2048]{1,0:T(8,128)(2,1)} fusion(bf16[128,256]{0,1:T(8,128)(2,1)S(1)} %bitcast.39, bf16[256,2048]{1,0:T(8,128)(2,1)S(1)} %copy-done), kind=kOutput, calls=%fused_computation | convolution fusion | flops 134479872 | bytes 1638400 | tf_op jit(solution)/shard_map/dot_general | solution.py:82
  50.8 0.0 reduce-scatter.2.cloned.1.call-update
  50.8 22.4 %reduce-scatter.2.cloned.1.call-done = bf16[128,512]{1,0:T(8,128)(2,1)} async-done(((bf16[128,2048]{1,0:T(8,128)(2,1)}), bf16[128,512]{1,0:T(8,128)(2,1)}) %reduce-scatter.2.cloned.1.call-update) | async-done | bytes 131088 | tf_op jit(solution)/shard_map/reduce_scatter | solution.py:83
  73.2 0.0 copy-done.1
  73.2 1.6 %add_convert_fusion = bf16[128,512]{1,0:T(8,128)(2,1)} fusion(bf16[128,512]{1,0:T(8,128)(2,1)} %reduce-scatter.2.cloned.1.call-done, bf16[128,512]{1,0:T(8,128)(2,1)S(1)} %copy-done.1), kind=kLoop, calls=%fused_computation.22 | loop fusion | flops 262144 | bytes 393216 | tf_op jit(solution)/shard_map/convert_element_type | solution.py:86
  (10 shorter events, 0.0 us)
Async XLA Ops:
  6.5 43.1 %copy-start = (bf16[256,2048]{1,0:T(8,128)(2,1)S(1)}, bf16[256,2048]{1,0:T(8,128)(2,1)}, u32[]{:S(2)}) copy-start(bf16[256,2048]{1,0:T(8,128)(2,1)} %param.13) | copy-start | bytes 3145732
  6.5 10.1 %copy-start.2 = (bf16[2048,256]{1,0:T(8,128)(2,1)S(1)}, bf16[2048,256]{1,0:T(8,128)(2,1)}, u32[]{:S(2)}) copy-start(bf16[2048,256]{1,0:T(8,128)(2,1)} %param.10) | copy-start | bytes 3145732
  6.5 66.6 %reduce-scatter.2.cloned.1.call-start = ((), (), s32[]{:S(2)}) async-start(), calls=%async_computation.1 | async-start | bytes 655360 | tf_op jit(solution)/shard_map/reduce_scatter | solution.py:83
  16.4 0.7 copy-start.5
  17.1 1.2 %copy-start.3 = (bf16[2048,256]{1,0:T(8,128)(2,1)S(1)}, bf16[2048,256]{1,0:T(8,128)(2,1)}, u32[]{:S(2)}) copy-start(bf16[2048,256]{1,0:T(8,128)(2,1)} %param.11) | copy-start | bytes 3145732
  18.3 1.2 %copy-start.4 = (bf16[2048,256]{1,0:T(8,128)(2,1)S(1)}, bf16[2048,256]{1,0:T(8,128)(2,1)}, u32[]{:S(2)}) copy-start(bf16[2048,256]{1,0:T(8,128)(2,1)} %param.9) | copy-start | bytes 3145732
  50.8 22.4 %copy-start.1 = (bf16[128,512]{1,0:T(8,128)(2,1)S(1)}, bf16[128,512]{1,0:T(8,128)(2,1)}, u32[]{:S(2)}) copy-start(bf16[128,512]{1,0:T(8,128)(2,1)} %param.7) | copy-start | bytes 393220
Sparse Core Ops, SparseCore 0:
  50.9 22.2 reduce-scatter.1
where the time goes:
time: 81.9 us; the launch traced here: 81.6 us
  blocking collectives  37.6 us (46%)
  waiting for transfers between devices  22.4 us (27%)
  between operations  13.5 us (16%)
  other arithmetic  3.1 us (4%)
  matrix products  2.85 us (3%)
  local copies, waits for them, and re-layouts  2.25 us (3%)
    reduce_scatter x1, waiting for transfers between devices, per_device(): lax.psum_scatter(partial_sums.astype(jnp.bfloat16), 'mp', scatter_dimensi...  22.4 us
    all_gather x1, blocking collectives, per_device(): lax.all_gather(key_rows, 'seq', axis=0, tiled=True)  14.6 us
    all_gather x1, blocking collectives, per_device(): lax.all_gather(value_rows, 'seq', axis=0, tiled=True)  14.1 us
    all_gather x1, blocking collectives, per_device(): full_rows = lax.all_gather(node_vectors, 'mp', axis=1, tiled=True)  8.84 us
    unnamed x12, local copies, waits for them, and re-layouts  2.11 us
  transfers between devices with their start and end apart: 1, of which 1 were waited for; matrix products, arithmetic and copies ran while one was open for 0% of the time, Pallas kernels for 0%

commit v1 on v0

--- a/solution.py
+++ b/solution.py
@@ -3,6 +3,23 @@
 import jax.numpy as jnp
 from jax import lax
 from jax.sharding import PartitionSpec as P
+
+
+def in_order(parts, dim):
+    parts = jnp.moveaxis(parts, 0, dim)
+    shape = parts.shape
+    return parts.reshape(*shape[:dim], shape[dim] * shape[dim + 1], *shape[dim + 2 :])
+
+
+def gather_around(array, axis, dim):
+    size = lax.axis_size(axis)
+    upward = [(i, (i + 1) % size) for i in range(size)]
+    blocks = [array]
+    while len(blocks) < size:
+        blocks.append(lax.ppermute(blocks[-1], axis, upward))
+    index = lax.axis_index(axis)
+    blocks = jnp.stack(blocks)[(index - jnp.arange(size)) % size]
+    return in_order(blocks, dim)
 
 
 def attend(state_in, blocks, query_heads, inverse_root_span, resident_groups, channel_span):
@@ -64,10 +81,7 @@
     )
     final = attend(
         initial,
-        (
-            lax.all_gather(key_rows, "seq", axis=0, tiled=True),
-            lax.all_gather(value_rows, "seq", axis=0, tiled=True),
-        ),
+        (lax.all_gather(key_rows, "seq", axis=0, tiled=True), gather_around(value_rows, "seq", 0)),
         query_heads,
         inverse_root_span,
         resident_groups,

time: 81.9 us -> 77.3 us (0.944)
  blocking collectives: 37.6 us -> 23.1 us
  waiting for transfers between devices: 22.4 us -> 30.5 us
  starting transfers between devices: 0.01 us -> 2.93 us
    all_gather x1 -> x0, blocking collectives: 14.1 us -> none  [per_device(): lax.all_gather(value_rows, 'seq', axis=0, tiled=True)]
    ppermute x0 -> x3, waiting for transfers between devices: none -> 10.9 us  [gather_around(): blocks.append(lax.ppermute(blocks[-1], axis, upward))]
    ppermute x0 -> x3, starting transfers between devices: none -> 2.93 us  [gather_around(): blocks.append(lax.ppermute(blocks[-1], axis, upward))]
    reduce_scatter x1, waiting for transfers between devices: 22.4 us -> 19.6 us  [per_device(): lax.psum_scatter(partial_sums.astype(jnp.bfloat16), 'mp', scatter_dimensi...]
    unnamed x12 -> x14, local copies, waits for them, and re-layouts: 2.11 us -> 1.25 us
  transfers between devices with their start and end apart: 1 -> 4, of which waited for: 1 -> 3; matrix products, arithmetic and copies ran while one was open for 0% -> 2% of each run, Pallas kernels for 0% -> 0%
where the time goes in v1:
time: 77.3 us; the launch traced here: 77.1 us
  waiting for transfers between devices  30.5 us (39%)
  blocking collectives  23.1 us (30%)
  between operations  13.5 us (17%)
  starting transfers between devices  2.93 us (4%)
  matrix products  2.87 us (4%)
  other arithmetic  2.35 us (3%)
  local copies, waits for them, and re-layouts  1.88 us (2%)
    reduce_scatter x1, waiting for transfers between devices, per_device(): lax.psum_scatter(partial_sums.astype(jnp.bfloat16), 'mp', scatter_dimensi...  19.6 us
    all_gather x1, blocking collectives, per_device(): lax.all_gather(key_rows, 'seq', axis=0, tiled=True)  14.1 us
    ppermute x3, waiting for transfers between devices, gather_around(): blocks.append(lax.ppermute(blocks[-1], axis, upward))  10.9 us
    all_gather x1, blocking collectives, per_device(): full_rows = lax.all_gather(node_vectors, 'mp', axis=1, tiled=True)  8.97 us
    ppermute x3, starting transfers between devices, gather_around(): blocks.append(lax.ppermute(blocks[-1], axis, upward))  2.93 us
    convert_element_type x1, other arithmetic, per_device(): return (node_vectors.astype(jnp.float32) + summed).astype(jnp.bfloat16)  1.59 us
  transfers between devices with their start and end apart: 4, of which 3 were waited for; matrix products, arithmetic and copies ran while one was open for 2% of the time, Pallas kernels for 0%

profile of v1, /device:TPU:0, one launch (start us, length us, event | category | flops | bytes accessed | tf_op | source)
XLA Modules:
  0.0 77.1 jit_solution(11828307231579773752)
XLA Ops:
  6.5 9.0 %all_gather.6 = bf16[128,2048]{1,0:T(8,128)(2,1)S(1)} all-gather(bf16[128,512]{1,0:T(8,128)(2,1)} %param.7), channel_id=1, replica_groups=mesh['groups'=2,'seq'=4,'mp'=4] {'mp'}, dimensions={1}, use_global_device_ids=true | all-gather | bytes 655360 | tf_op jit(solution)/shard_map/all_gather | solution.py:58
  15.5 0.2 convert_reduce_fusion
  15.7 0.3 fusion.6
  16.0 0.4 copy-done.5
  16.4 0.4 convolution_convert_fusion.1
  16.7 1.6 %collective-permute-start = (bf16[128,256]{1,0:T(8,128)(2,1)S(1)}, bf16[128,256]{1,0:T(8,128)(2,1)S(1)}, u32[]{:S(2)}, u32[]{:S(2)}) collective-permute-start(bf16[128,256]{1,0:T(8,128)(2,1)S(1)} %convolution_convert_fusion.1), channel_id=1, source_target_pairs={{0,4},{4,8},{8,12},{12,0},{1,5},{5,9},{9,13},{13,1},{2,6},{6,10},{... | collective-permute-start | bytes 196616 | tf_op jit(solution)/shard_map/ppermute | solution.py:19
  18.4 0.4 convolution_convert_fusion.2
  18.8 0.8 %copy-done.4 = bf16[2048,256]{1,0:T(8,128)(2,1)S(1)} copy-done((bf16[2048,256]{1,0:T(8,128)(2,1)S(1)}, bf16[2048,256]{1,0:T(8,128)(2,1)}, u32[]{:S(2)}) %copy-start.4) | copy-done | bytes 1048600
  19.6 0.4 fusion.5
  20.0 14.1 %all_gather.7 = bf16[512,256]{1,0:T(8,128)(2,1)S(1)} all-gather(bf16[128,256]{1,0:T(8,128)(2,1)S(1)} %convolution_convert_fusion.2), channel_id=1, replica_groups=mesh['groups'=2,'seq'=4,'mp'=4] {'seq'}, dimensions={0}, use_global_device_ids=true | all-gather | bytes 327680 | tf_op jit(solution)/shard_map/all_gather | solution.py:84
  34.1 0.3 fusion.23
  34.4 0.2 fusion.9
  34.7 0.0 collective-permute-done
  34.7 1.3 %collective-permute-start.1 = (bf16[128,256]{1,0:T(8,128)(2,1)S(1)}, bf16[128,256]{1,0:T(8,128)(2,1)S(1)}, u32[]{:S(2)}, u32[]{:S(2)}) collective-permute-start(bf16[128,256]{1,0:T(8,128)(2,1)S(1)} %collective-permute-done), channel_id=1, source_target_pairs={{0,4},{4,8},{8,12},{12,0},{1,5},{5,9},{9,13},{13,1},{2,6},{6,10},{... | collective-permute-start | bytes 196616 | tf_op jit(solution)/shard_map/ppermute | solution.py:19
  36.0 4.8 %collective-permute-done.1 = bf16[128,256]{1,0:T(8,128)(2,1)S(1)} collective-permute-done((bf16[128,256]{1,0:T(8,128)(2,1)S(1)}, bf16[128,256]{1,0:T(8,128)(2,1)S(1)}, u32[]{:S(2)}, u32[]{:S(2)}) %collective-permute-start.1) | collective-permute-done | bytes 65568 | tf_op jit(solution)/shard_map/ppermute | solution.py:19
  40.8 0.0 collective-permute-start.2
  40.8 6.1 %collective-permute-done.2 = bf16[128,256]{1,0:T(8,128)(2,1)S(1)} collective-permute-done((bf16[128,256]{1,0:T(8,128)(2,1)S(1)}, bf16[128,256]{1,0:T(8,128)(2,1)S(1)}, u32[]{:S(2)}, u32[]{:S(2)}) %collective-permute-start.2) | collective-permute-done | bytes 65568 | tf_op jit(solution)/shard_map/ppermute | solution.py:19
  46.9 0.6 gather_fusion
  47.5 0.1 reshape_reshape.3
  47.5 0.3 fusion.4
  47.9 1.1 %convolution_convert_fusion = bf16[128,2048]{1,0:T(8,128)(2,1)} fusion(bf16[128,256]{0,1:T(8,128)(2,1)S(1)} %bitcast.42, bf16[256,2048]{1,0:T(8,128)(2,1)S(1)} %copy-done), kind=kOutput, calls=%fused_computation.1 | convolution fusion | flops 134479872 | bytes 1638400 | tf_op jit(solution)/shard_map/dot_general | solution.py:96
  49.0 0.0 reduce-scatter.2.cloned.1.call-update
  49.0 19.6 %reduce-scatter.2.cloned.1.call-done = bf16[128,512]{1,0:T(8,128)(2,1)} async-done(((bf16[128,2048]{1,0:T(8,128)(2,1)}), bf16[128,512]{1,0:T(8,128)(2,1)}) %reduce-scatter.2.cloned.1.call-update) | async-done | bytes 131088 | tf_op jit(solution)/shard_map/reduce_scatter | solution.py:97
  68.6 1.6 %add_convert_fusion = bf16[128,512]{1,0:T(8,128)(2,1)} fusion(bf16[128,512]{1,0:T(8,128)(2,1)} %reduce-scatter.2.cloned.1.call-done, bf16[128,512]{1,0:T(8,128)(2,1)S(1)} %copy-done.1), kind=kLoop, calls=%fused_computation.25 | loop fusion | flops 262144 | bytes 393216 | tf_op jit(solution)/shard_map/convert_element_type | solution.py:100
  (21 shorter events, 0.1 us)
Async XLA Ops:
  6.5 41.3 %copy-start = (bf16[256,2048]{1,0:T(8,128)(2,1)S(1)}, bf16[256,2048]{1,0:T(8,128)(2,1)}, u32[]{:S(2)}) copy-start(bf16[256,2048]{1,0:T(8,128)(2,1)} %param.13) | copy-start | bytes 3145732
  6.5 9.4 %copy-start.2 = (bf16[2048,256]{1,0:T(8,128)(2,1)S(1)}, bf16[2048,256]{1,0:T(8,128)(2,1)}, u32[]{:S(2)}) copy-start(bf16[2048,256]{1,0:T(8,128)(2,1)} %param.11) | copy-start | bytes 3145732
  6.5 62.1 %reduce-scatter.2.cloned.1.call-start = ((), (), s32[]{:S(2)}) async-start(), calls=%async_computation.1 | async-start | bytes 655360 | tf_op jit(solution)/shard_map/reduce_scatter | solution.py:97
  15.7 0.7 copy-start.5
  16.4 2.0 %copy-start.6 = (f32[2]{0:T(128)S(1)}, f32[2]{0:T(128)}, u32[]{:S(2)}) copy-start(f32[2]{0:T(128)} %param.12) | copy-start | bytes 28
  16.4 2.0 %copy-start.3 = (bf16[2048,256]{1,0:T(8,128)(2,1)S(1)}, bf16[2048,256]{1,0:T(8,128)(2,1)}, u32[]{:S(2)}) copy-start(bf16[2048,256]{1,0:T(8,128)(2,1)} %param.10) | copy-start | bytes 3145732
  16.7 17.9 %collective-permute-start = (bf16[128,256]{1,0:T(8,128)(2,1)S(1)}, bf16[128,256]{1,0:T(8,128)(2,1)S(1)}, u32[]{:S(2)}, u32[]{:S(2)}) collective-permute-start(bf16[128,256]{1,0:T(8,128)(2,1)S(1)} %convolution_convert_fusion.1), channel_id=1, source_target_pairs={{0,4},{4,8},{8,12},{12,0},{1,5},{5,9},{9,13},{13,1},{2,6},{6,10},{... | collective-permute-start | bytes 196616 | tf_op jit(solution)/shard_map/ppermute | solution.py:19
  18.4 1.2 %copy-start.4 = (bf16[2048,256]{1,0:T(8,128)(2,1)S(1)}, bf16[2048,256]{1,0:T(8,128)(2,1)}, u32[]{:S(2)}) copy-start(bf16[2048,256]{1,0:T(8,128)(2,1)} %param.9) | copy-start | bytes 3145732
  34.7 6.1 %collective-permute-start.1 = (bf16[128,256]{1,0:T(8,128)(2,1)S(1)}, bf16[128,256]{1,0:T(8,128)(2,1)S(1)}, u32[]{:S(2)}, u32[]{:S(2)}) collective-permute-start(bf16[128,256]{1,0:T(8,128)(2,1)S(1)} %collective-permute-done), channel_id=1, source_target_pairs={{0,4},{4,8},{8,12},{12,0},{1,5},{5,9},{9,13},{13,1},{2,6},{6,10},{... | collective-permute-start | bytes 196616 | tf_op jit(solution)/shard_map/ppermute | solution.py:19
  40.8 6.1 %collective-permute-start.2 = (bf16[128,256]{1,0:T(8,128)(2,1)S(1)}, bf16[128,256]{1,0:T(8,128)(2,1)S(1)}, u32[]{:S(2)}, u32[]{:S(2)}) collective-permute-start(bf16[128,256]{1,0:T(8,128)(2,1)S(1)} %collective-permute-done.1), channel_id=1, source_target_pairs={{0,4},{4,8},{8,12},{12,0},{1,5},{5,9},{9,13},{13,1},{2,6},{6,10},{... | collective-permute-start | bytes 196616 | tf_op jit(solution)/shard_map/ppermute | solution.py:19
  49.0 19.7 %copy-start.1 = (bf16[128,512]{1,0:T(8,128)(2,1)S(1)}, bf16[128,512]{1,0:T(8,128)(2,1)}, u32[]{:S(2)}) copy-start(bf16[128,512]{1,0:T(8,128)(2,1)} %param.7) | copy-start | bytes 393220
Sparse Core Ops, SparseCore 0:
  49.1 19.4 reduce-scatter.1
